TPU v7x, 32 devices: a whole 2x2x4 slice. The times are simulated.
32 devices in a mesh: grp: 2 (over z_hi), seq: 8 (over y, x, core), tp: 2 (over z_lo).
Axes of the slice: x: 2, y: 2, z: 4 (z_hi: 2, z_lo: 2; z = z_hi * 2 + z_lo), core: 2. Of those that a mesh axis runs over, the one named last changes fastest.
Arguments:
- latents: bfloat16 [2, 64, 2048], P('grp', None, 'seq'), may hold values from -6 to 6
- patch_weight: bfloat16 [128, 5120], replicated, may hold values from -0.5 to 0.5
- patch_bias: float32 [5120], replicated, may hold values from -3 to 3
- modulation: float32 [3, 5120], replicated, may hold values from -3 to 3
- qkv_weight: bfloat16 [5120, 3, 1024], P(None, None, 'seq'), may hold values from -0.078125 to 0.078125
- norm_gain: float32 [2, 1024], P(None, 'seq'), may hold values from 0.5 to 16
- out_weight: bfloat16 [1024, 5120], P('seq', ('grp', 'tp')), may hold values from -0.5 to 0.5
- token_order: int32 [2048], replicated, may hold values from 0 to 2047, each once
- window_start: int32 [1], replicated, may hold values from 0 to 1024
Outputs:
- attended: bfloat16 [1024, 5120], P('seq', ('grp', 'tp'))
Inputs may be any that keep to these rules, and one draw needn't show every extreme that they name: Position j of the target layout holds frame-major token token_order[j]; every token stands once. The window covers target positions window_start[0] to window_start[0] + 1023.
All inputs are finite; a program needn't handle non-finite values.
Results may differ from a plain program's by a relative error of at most 0.018.
The roundings to bfloat16 on the way count: a program that leaves them out, or rounds other values in their place, can miss the bound.
Values may be sent and summed in bfloat16 or wider, within the bound.
A program may use at most 128 MiB of HBM per device.

v0:
```python
import math

import jax
import jax.numpy as jnp
from jax import lax
from jax.sharding import PartitionSpec as P

QW_DEV = 128


norm_eps = 0.1


def swapped(block, axis, apart):
    count = lax.axis_size(axis)
    route = []
    for low in range(count):
        high = low | 1 << apart
        if high != low and high < count:
            route += [(low, high), (high, low)]
    return lax.ppermute(block, axis, route)


def joined(array, axis, combine):
    everything = jax.tree.map(lambda part: lax.all_gather(part, axis), array)
    initial = jax.tree.map(lambda part: part[0], everything)

    def step(k, so_far):
        return combine(so_far, jax.tree.map(lambda part: part[k], everything))

    return lax.fori_loop(1, lax.axis_size(axis), step, initial)


def embed_rows(columns, patch_weight, patch_bias, modulation):
    channels = columns.shape[1]
    weight = patch_weight.reshape(2, channels, patch_weight.shape[1])
    embedded = (
        lax.dot_general(
            columns, weight, (((0, 1), (0, 1)), ((), ())), preferred_element_type=jnp.float32
        )
        + patch_bias
    )
    centre = embedded - jnp.mean(embedded, axis=1, keepdims=True)
    spread = jnp.mean(centre * centre, axis=1, keepdims=True)
    normed = centre * lax.rsqrt(spread + norm_eps) * (1.0 + modulation[1]) + modulation[0]
    return normed.astype(jnp.bfloat16)


def project_rows(columns, flat_weight, patch_weight, patch_bias, modulation):
    row_total = columns.shape[2]
    block = math.gcd(row_total, 512)

    def one_block(block_index):
        section = lax.dynamic_slice_in_dim(columns, block_index * block, block, 2)
        normed = embed_rows(section, patch_weight, patch_bias, modulation)
        return jnp.dot(normed, flat_weight, preferred_element_type=jnp.float32)

    result = lax.map(one_block, jnp.arange(row_total // block))
    return result.reshape(row_total, flat_weight.shape[1])


def per_device(
    latents,
    patch_weight,
    patch_bias,
    modulation,
    qkv_weight,
    norm_gain,
    out_weight,
    token_order,
    window_start,
):
    head_dim = qkv_weight.shape[2]
    seq_count = lax.axis_size("seq")
    groups = lax.axis_size("grp") * lax.axis_size("tp")
    quarter = lax.axis_index("grp") * lax.axis_size("tp") + lax.axis_index("tp")
    partner = swapped(latents, "grp", 0)
    is_high = lax.axis_index("grp") == 0
    paired = jnp.where(
        is_high, jnp.concatenate([latents, partner], 0), jnp.concatenate([partner, latents], 0)
    )
    gathered = lax.all_gather(paired, "seq", axis=2, tiled=True)
    tokens = gathered.shape[2]
    key_count = tokens // groups
    flat_weight = qkv_weight.reshape(qkv_weight.shape[0], 3 * head_dim)
    key_columns = lax.dynamic_slice_in_dim(gathered, quarter * key_count, key_count, 2)
    pair_raw = project_rows(
        key_columns, flat_weight[:, head_dim:], patch_weight, patch_bias, modulation
    )
    key_raw = pair_raw[:, :head_dim]
    values = pair_raw[:, head_dim:].astype(jnp.bfloat16)
    window_len = QW_DEV * seq_count
    window_rows = lax.dynamic_slice_in_dim(token_order, window_start[0], window_len)
    part_len = window_len // groups
    query_rows = lax.dynamic_slice_in_dim(window_rows, quarter * part_len, part_len)
    query_columns = jnp.take(gathered, query_rows, axis=2)
    query_raw = project_rows(
        query_columns, flat_weight[:, :head_dim], patch_weight, patch_bias, modulation
    )
    query_total, key_total = lax.psum(
        (jnp.sum(query_raw * query_raw, axis=1), jnp.sum(key_raw * key_raw, axis=1)), "seq"
    )
    norm_width = head_dim * seq_count
    queries = (
        query_raw * lax.rsqrt(query_total[:, None] / norm_width + norm_eps) * norm_gain[0]
    ).astype(jnp.bfloat16)
    key_rows = (
        key_raw * lax.rsqrt(key_total[:, None] / norm_width + norm_eps) * norm_gain[1]
    ).astype(jnp.bfloat16)
    queries = lax.all_gather(queries, ("grp", "tp"), axis=0, tiled=True)
    query_len = queries.shape[0]
    query_block = math.gcd(query_len, 512)
    score_scale = head_dim ** (-0.5)

    def attend(block_index):
        query_part = lax.dynamic_slice_in_dim(queries, block_index * query_block, query_block, 0)
        scores = (
            lax.dot_general(
                query_part, key_rows, (((1,), (1,)), ((), ())), preferred_element_type=jnp.float32
            )
            * score_scale
        )
        row_max = jnp.max(scores, axis=1)
        probs = jnp.exp(scores - row_max[:, None])
        row_sum = jnp.sum(probs, axis=1)
        row_acc = jnp.dot(probs.astype(jnp.bfloat16), values, preferred_element_type=jnp.float32)
        return (row_max, row_sum, row_acc)

    maxima, sums, accums = lax.map(attend, jnp.arange(query_len // query_block))
    maxima = maxima.reshape(query_len)
    sums = sums.reshape(query_len)
    accums = accums.reshape(query_len, head_dim)

    def combine(first, second):
        row_max = jnp.maximum(first[0], second[0])
        first_factor = jnp.exp(first[0] - row_max)
        second_factor = jnp.exp(second[0] - row_max)
        row_sum = first[1] * first_factor + second[1] * second_factor
        row_acc = first[2] * first_factor[:, None] + second[2] * second_factor[:, None]
        return (row_max, row_sum, row_acc)

    row_max, row_sum, row_acc = joined((maxima, sums, accums), ("grp", "tp"), combine)
    attention = (row_acc / row_sum[:, None]).astype(jnp.bfloat16)
    cols_dev = out_weight.shape[1]
    gate_cols = lax.dynamic_slice_in_dim(modulation[2], quarter * cols_dev, cols_dev)
    regrouped = lax.all_to_all(attention, "seq", split_axis=0, concat_axis=1, tiled=True)
    mixed_out = jnp.dot(
        regrouped,
        lax.all_gather(out_weight, "seq", axis=0, tiled=True),
        preferred_element_type=jnp.float32,
    )
    return (mixed_out * gate_cols).astype(jnp.bfloat16)


def solution(mesh):
    in_specs = (
        P("grp", None, "seq"),
        P(),
        P(),
        P(),
        P(None, None, "seq"),
        P(None, "seq"),
        P("seq", ("grp", "tp")),
        P(),
        P(),
    )
    out_specs = P("seq", ("grp", "tp"))
    return jax.shard_map(
        per_device, mesh=mesh, in_specs=in_specs, out_specs=out_specs, check_vma=False
    )
```

profile of v0, /device:TPU:9, one launch (start us, length us, event | category | flops | bytes accessed | tf_op | source)
XLA Modules:
  0.0 167.8 jit_solution(8679716140680726561)
XLA Ops:
  6.5 2.4 %collective-permute-start = (bf16[1,64,256]{2,1,0:T(8,128)(2,1)}, bf16[1,64,256]{2,1,0:T(8,128)(2,1)S(1)}, u32[]{:S(2)}, u32[]{:S(2)}) collective-permute-start(bf16[1,64,256]{2,1,0:T(8,128)(2,1)} %param.13), channel_id=1, source_target_pairs={{0,16},{16,0},{1,17},{17,1},{2,18},{18,2},{3,19},{19,3},{4,20},{20... | collective-permute-start | bytes 98312 | tf_op jit(solution)/shard_map/ppermute | solution.py:21
  9.6 1.7 %fusion.22 = (f32[1,5120]{1,0:T(1,128)}, f32[1,5120]{1,0:T(1,128)S(1)}, f32[1,5120]{1,0:T(1,128)S(1)}) fusion(f32[3,5120]{1,0:T(4,128)} %param.16), kind=kLoop, calls=%fused_computation.62 | loop fusion | flops 5120 | bytes 122880 | tf_op jit(solution)/shard_map/slice | solution.py:145
  11.3 1.3 slice_bitcast_fusion.1
  12.6 1.2 compare_and_fusion
  13.9 6.3 %copy.28 = bf16[5120,3,128]{0,2,1:T(8,128)(2,1)} copy(bf16[5120,3,128]{2,0,1:T(8,128)(2,1)} %param.17) | data formatting | bytes 7864320 | tf_op args[4]
  20.3 11.7 %all_gather.18 = bf16[2,64,2048]{2,1,0:T(8,128)(2,1)S(1)} all-gather(bf16[2,64,256]{2,1,0:T(8,128)(2,1)S(1)} %maximum_select_fusion), channel_id=1, replica_groups=mesh['grp'=2,'seq'=8,'tp'=2] {'seq'}, dimensions={2}, use_global_device_ids=true | all-gather | bytes 589824 | tf_op jit(solution)/shard_map/all_gather | solution.py:82
  32.0 0.7 copy.26
  32.8 1.7 fusion.9
  34.4 1.6 multiply_reduce_fusion
  36.5 2.5 %fusion.11 = f32[512,256]{0,1:T(8,128)S(1)} fusion(f32[512,5120,1]{1,0,2:T(8,128)S(1)} %get-tuple-element.357, f32[5120]{0:T(1024)S(1)} %bitcast.97, f32[5120]{0:T(1024)S(1)} %bitcast.95, f32[512]{0:T(512)S(1)} %add_rsqrt_fusion.1, f32[512]{0:T(512)S(1)} %broadcast_multiply_fusion, f32[5120]{0:T(1024)S(1)} %copy-done.3, bf16[5120,384]{0,1:T(8,128)(2,1)S(1)} %bitcast.83), kind=kOutput, calls=%fused_computation.26 | convolution fusion | flops 1357905920 | bytes 13697024 | tf_op jit(solution)/shard_map/while/body/eval_jaxpr/dot_general | solution.py:56
  39.1 1.6 gather_fusion
  40.7 1.2 fusion.19
  42.0 1.7 %fusion.23 = (f32[256]{0:T(256)S(1)}, f32[256,5120]{1,0:T(8,128)S(1)}) fusion(f32[5120]{0:T(1024)} %param.15, bf16[2,64,5120]{2,1,0:T(8,128)(2,1)S(1)} %bitcast.80, bf16[2,64,256]{1,0,2:T(2,128)(2,1)S(1)} %fusion.19), kind=kOutput, calls=%fused_computation.63 | convolution fusion | flops 338165504 | bytes 6640640 | tf_op jit(solution)/shard_map/while/body/eval_jaxpr/dot_general | solution.py:38
  44.4 2.6 %multiply_reduce_fusion.3 = (f32[256]{0:T(256)S(1)}, f32[256,128]{0,1:T(8,128)S(1)}) fusion(bf16[5120,384]{0,1:T(8,128)(2,1)} %bitcast.82, f32[256,5120]{1,0:T(8,128)S(1)} %get-tuple-element.353, f32[5120]{0:T(1024)S(1)} %bitcast.98, f32[5120]{0:T(1024)S(1)} %bitcast.96, f32[256]{0:T(256)S(1)} %add_rsqrt_fusion.3, f32[256]{0:T(256)S(1)} %broadcast_multiply_fusion.1), kind=kOutput, calls=%fused_computation.42 | convolution fusion | flops 342163200 | bytes 6728704 | tf_op jit(solution)/shard_map/while/body/eval_jaxpr/dot_general | solution.py:56
  47.0 11.3 %all-reduce = (f32[256]{0:T(256)S(1)}, f32[512]{0:T(512)S(1)}) all-reduce(f32[256]{0:T(256)S(1)} %get-tuple-element.354, f32[512]{0:T(512)S(1)} %multiply_reduce_fusion.2), channel_id=1, replica_groups=mesh['grp'=2,'seq'=8,'tp'=2] {'seq'}, use_global_device_ids=true, to_apply=%region_3.4 | all-reduce | flops 768 | bytes 6144 | tf_op jit(solution)/shard_map/psum | solution.py:100
  58.6 10.1 %all_gather.19 = bf16[1024,128]{0,1:T(8,128)(2,1)S(1)} all-gather(bf16[256,128]{0,1:T(8,128)(2,1)S(1)} %multiply_convert_fusion.1), channel_id=1, replica_groups=mesh['grp'=2,'seq'=8,'tp'=2] {'grp','tp'}, dimensions={0}, use_global_device_ids=true | all-gather | bytes 327680 | tf_op jit(solution)/shard_map/all_gather | solution.py:110
  68.8 4.4 %while.11 = (s32[]{:T(128)}, f32[2,512]{1,0:T(2,128)S(1)}, f32[2,512]{1,0:T(2,128)S(1)}, f32[2,512,128]{2,1,0:T(8,128)S(1)}, s32[2]{0:T(128)S(1)}, /*index=5*/bf...) while((s32[]{:T(128)}, f32[2,512]{1,0:T(2,128)S(1)}, ...), condition=%wide.region_11.12_spmd, body=%wide.region_8.11_spmd.sunk | while | flops 135789568 | bytes 3817663 | solution.py:129
  73.3 0.8 copy-done.2
  74.9 10.3 %all-gather = f32[4,1,1024]{2,1,0:T(1,128)S(1)} all-gather(f32[1,1,1024]{2,1,0:T(1,128)S(1)} %reshape.73), channel_id=1, replica_groups=mesh['grp'=2,'seq'=8,'tp'=2] {'grp','tp'}, dimensions={0}, use_global_device_ids=true | all-gather | bytes 20480 | tf_op jit(solution)/shard_map/all_gather | solution.py:25
  85.2 11.1 %all-gather.1 = f32[4,1,1024]{2,1,0:T(1,128)S(1)} all-gather(f32[1,1,1024]{2,1,0:T(1,128)S(1)} %reshape.75), channel_id=1, replica_groups=mesh['grp'=2,'seq'=8,'tp'=2] {'grp','tp'}, dimensions={0}, use_global_device_ids=true | all-gather | bytes 20480 | tf_op jit(solution)/shard_map/all_gather | solution.py:25
  96.3 26.0 %all-gather.5.cloned.1.call-done = f32[4,1024,128]{2,1,0:T(8,128)} async-done(((f32[1,1024,128]{2,1,0:T(8,128)}), f32[4,1024,128]{2,1,0:T(8,128)}) %all-gather.5.cloned.1.call-update) | async-done | bytes 2097168 | tf_op jit(solution)/shard_map/all_gather | solution.py:25
  122.2 1.1 slice_bitcast_fusion
  123.3 4.7 %while.42 = (s32[]{:T(128)}, f32[1024]{0:T(1024)S(1)}, f32[1024]{0:T(1024)S(1)}, f32[1024,128]{1,0:T(8,128)S(1)}, f32[4,1024]{1,0:T(4,128)S(1)}, /*index=5*/f32[...) while((s32[]{:T(128)}, f32[1024]{0:T(1024)S(1)}, f32[1024]{0:T(1024)S(1)}, ...), condition=%wide.region_13.14_spmd, body=%wide.region_12.13_spmd.sunk | while | flops 399365 | bytes 1630359 | solution.py:31
  123.4 1.5 fusion.43
  124.9 1.5 fusion.43
  126.5 1.5 fusion.43
  128.0 0.9 divide_convert_fusion
  128.9 4.8 %all-to-all-start = ((bf16[8,128,128]{2,1,0:T(8,128)(2,1)}), bf16[8,128,128]{2,1,0:T(8,128)(2,1)S(1)}, u32[]{:S(2)}, u32[]{:S(2)}) async-start(bf16[8,128,128]{2,1,0:T(8,128)(2,1)} %bitcast.21), calls=%async_computation | async-start | bytes 524288 | tf_op jit(solution)/shard_map/all_to_all | solution.py:146
  133.7 0.7 dynamic-slice_reduce_fusion
  134.4 6.1 %all-to-all-done = bf16[8,128,128]{2,1,0:T(8,128)(2,1)S(1)} async-done(((bf16[8,128,128]{2,1,0:T(8,128)(2,1)}), bf16[8,128,128]{2,1,0:T(8,128)(2,1)S(1)}, u32[]{:S(2)}, u32[]{:S(2)}) %all-to-all-start) | async-done | bytes 262176 | tf_op jit(solution)/shard_map/all_to_all | solution.py:146
  140.7 17.2 %all-gather.7.cloned.1.call-done = bf16[1024,1280]{1,0:T(8,128)(2,1)} async-done(((bf16[128,1280]{1,0:T(8,128)(2,1)}), bf16[1024,1280]{1,0:T(8,128)(2,1)}) %all-gather.7.cloned.1.call-update) | async-done | bytes 2621456 | tf_op jit(solution)/shard_map/all_gather | solution.py:149
  157.9 3.0 %fusion.14 = bf16[128,1280]{1,0:T(8,128)(2,1)} fusion(bf16[128,1024]{0,1:T(8,128)(2,1)S(1)} %bitcast.84, bf16[1024,1280]{1,0:T(8,128)(2,1)} %all-gather.7.cloned.1.call-done, f32[1280]{0:T(1024)S(1)} %dynamic-slice_reduce_fusion), kind=kOutput, calls=%fused_computation.30 | convolution fusion | flops 335872000 | bytes 3216384 | tf_op jit(solution)/shard_map/dot_general | solution.py:147
  (70 shorter events, 5.8 us)
Async XLA Ops:
  6.5 26.2 %copy-start = (bf16[128,5120]{1,0:T(8,128)(2,1)S(1)}, bf16[128,5120]{1,0:T(8,128)(2,1)}, u32[]{:S(2)}) copy-start(bf16[128,5120]{1,0:T(8,128)(2,1)} %param.14) | copy-start | bytes 3932164
  6.5 13.7 %copy-start.4 = (bf16[1,64,256]{2,1,0:T(8,128)(2,1)S(1)}, bf16[1,64,256]{2,1,0:T(8,128)(2,1)}, u32[]{:S(2)}) copy-start(bf16[1,64,256]{2,1,0:T(8,128)(2,1)} %param.13) | copy-start | bytes 98308
  6.5 26.2 %copy-start.3 = (f32[5120]{0:T(1024)S(1)}, f32[5120]{0:T(1024)}, u32[]{:S(2)}) copy-start(f32[5120]{0:T(1024)} %param.15) | copy-start | bytes 61444
  6.5 115.7 %all-gather.5.cloned.1.call-start = ((), (), s32[]{:S(2)}) async-start(), calls=%async_computation.1 | async-start | bytes 2621440 | tf_op jit(solution)/shard_map/all_gather | solution.py:25
  6.5 13.7 %collective-permute-start = (bf16[1,64,256]{2,1,0:T(8,128)(2,1)}, bf16[1,64,256]{2,1,0:T(8,128)(2,1)S(1)}, u32[]{:S(2)}, u32[]{:S(2)}) collective-permute-start(bf16[1,64,256]{2,1,0:T(8,128)(2,1)} %param.13), channel_id=1, source_target_pairs={{0,16},{16,0},{1,17},{17,1},{2,18},{18,2},{3,19},{19,3},{4,20},{20... | collective-permute-start | bytes 98312 | tf_op jit(solution)/shard_map/ppermute | solution.py:21
  11.3 24.7 %copy-start.5 = (f32[1,5120]{1,0:T(1,128)}, f32[1,5120]{1,0:T(1,128)S(1)}, u32[]{:S(2)}) copy-start(f32[1,5120]{1,0:T(1,128)S(1)} %get-tuple-element.348) | copy-start | bytes 61444
  11.3 24.7 %copy-start.7 = (f32[1,5120]{1,0:T(1,128)}, f32[1,5120]{1,0:T(1,128)S(1)}, u32[]{:S(2)}) copy-start(f32[1,5120]{1,0:T(1,128)S(1)} %get-tuple-element.349) | copy-start | bytes 61444
  34.4 2.1 %copy-start.1 = (bf16[5120,3,128]{0,2,1:T(8,128)(2,1)S(1)}, bf16[5120,3,128]{0,2,1:T(8,128)(2,1)}, u32[]{:S(2)}) copy-start(bf16[5120,3,128]{0,2,1:T(8,128)(2,1)} %copy.28) | copy-start | bytes 11796484
  41.9 2.4 %copy-start.6 = (f32[1,5120]{1,0:T(1,128)S(1)}, f32[1,5120]{1,0:T(1,128)}, u32[]{:S(2)}) copy-start(f32[1,5120]{1,0:T(1,128)} %copy-done.5) | copy-start | bytes 61444
  42.0 2.4 %copy-start.8 = (f32[1,5120]{1,0:T(1,128)S(1)}, f32[1,5120]{1,0:T(1,128)}, u32[]{:S(2)}) copy-start(f32[1,5120]{1,0:T(1,128)} %copy-done.7) | copy-start | bytes 61444
  44.3 13.9 %copy-start.10 = (f32[128]{0:T(128)S(1)}, f32[128]{0:T(128)}, u32[]{:S(2)}) copy-start(f32[128]{0:T(128)} %get-tuple-element.350) | copy-start | bytes 1540
  44.4 14.2 %copy-start.9 = (f32[128]{0:T(128)S(1)}, f32[128]{0:T(128)}, u32[]{:S(2)}) copy-start(f32[128]{0:T(128)} %get-tuple-element.351) | copy-start | bytes 1540
  73.2 0.8 copy-start.2
  74.1 83.8 %all-gather.7.cloned.1.call-start = ((), (), s32[]{:S(2)}) async-start(), calls=%async_computation.2 | async-start | bytes 2949120 | tf_op jit(solution)/shard_map/all_gather | solution.py:149
  128.9 11.6 %all-to-all-start = ((bf16[8,128,128]{2,1,0:T(8,128)(2,1)}), bf16[8,128,128]{2,1,0:T(8,128)(2,1)S(1)}, u32[]{:S(2)}, u32[]{:S(2)}) async-start(bf16[8,128,128]{2,1,0:T(8,128)(2,1)} %bitcast.21), calls=%async_computation | async-start | bytes 524288 | tf_op jit(solution)/shard_map/all_to_all | solution.py:146
Sparse Core Ops, SparseCore 0:
  74.2 47.9 all-gather.4
  124.1 33.7 all-gather.6
where the time goes:
time: 170 us; the launch traced here: 168 us
  blocking collectives  54.5 us (32%)
  waiting for transfers between devices  50 us (29%)
  local copies, waits for them, and re-layouts  15 us (9%)
  between operations  14.3 us (8%)
  matrix products  12.7 us (7%)
  other arithmetic  12.6 us (7%)
  starting transfers between devices  7.17 us (4%)
    all_gather x1, waiting for transfers between devices, joined(): everything = jax.tree.map(lambda part: lax.all_gather(part, axis), array)  26 us
    all_gather x2, blocking collectives, joined(): everything = jax.tree.map(lambda part: lax.all_gather(part, axis), array)  21.4 us
    all_gather x1, waiting for transfers between devices, per_device(): lax.all_gather(out_weight, 'seq', axis=0, tiled=True)  17.2 us
    all_gather x1, blocking collectives, per_device(): gathered = lax.all_gather(paired, 'seq', axis=2, tiled=True)  11.7 us
    psum x1, blocking collectives, per_device(): lax.psum((jnp.sum(query_raw * query_raw, axis=1), jnp.sum(key_raw * key_r...  11.3 us
    all_gather x1, blocking collectives, per_device(): queries = lax.all_gather(queries, ('grp', 'tp'), axis=0, tiled=True)  10.1 us
    unnamed x27, local copies, waits for them, and re-layouts  7.73 us
    all_to_all x1, waiting for transfers between devices, per_device(): lax.all_to_all(attention, 'seq', split_axis=0, concat_axis=1, tiled=True)  6.12 us
  transfers between devices with their start and end apart: 4, of which 3 were waited for; matrix products, arithmetic and copies ran while one was open for 11% of the time, Pallas kernels for 0%

commit v1 on v0

v1 whole, which is shorter than its diff:
```python
import jax
import jax.numpy as jnp
from jax import lax
from jax.experimental import pallas as pl
from jax.experimental.pallas import tpu as pltpu
from jax.sharding import PartitionSpec as P

QW_DEV = 128
norm_eps = 0.1
MESH = pl.DeviceIdType.MESH
F32 = jnp.float32
BF16 = jnp.bfloat16


def flipped(index, mask):
    bit = 1
    while bit <= mask:
        if mask & bit:
            index = index + bit * (1 - 2 * ((index // bit) % 2))
        bit *= 2
    return index


def three_parts(x):
    high = x.astype(BF16).astype(F32)
    rest = x - high
    middle = rest.astype(BF16).astype(F32)
    return high, middle, rest - middle


def kernel(
    lat, pw, pb, mod, wq, gain, ow, rows, out,
    lat_all, x_aug, w_aug, centre, q_raw, k_raw, v_t, k_low,
    ss_all, q_all, part_acc, part_stat, got_acc, got_stat, att_z, att_x, ow_all,
    lat_s, lat_f, lat_r, ow_s, ow_l, ow_r, ss_s, ss_r, q_s, q_r,
    acc_s, acc_r, stat_s, stat_r, az_s, az_r, ax_s, ax_r,
):
    grp, seq, tp = lax.axis_index("grp"), lax.axis_index("seq"), lax.axis_index("tp")
    seq_n, tp_n = lax.axis_size("seq"), lax.axis_size("tp")
    groups = lax.axis_size("grp") * tp_n
    quarter = grp * tp_n + tp
    channels, local = lat.shape[1], lat.shape[2]
    width = pw.shape[1]
    hd = k_raw.shape[1]
    key_n = k_raw.shape[0]
    query_n = q_raw.shape[0]
    owners = seq_n // groups
    cols = ow.shape[1]

    def plane(index):
        return {"grp": grp, "seq": index, "tp": tp}

    def column(index):
        return {"grp": index // tp_n, "seq": seq, "tp": index % tp_n}

    def send(src, dst, send_sem, recv_sem, device):
        return pltpu.make_async_remote_copy(
            src_ref=src, dst_ref=dst, send_sem=send_sem, recv_sem=recv_sem,
            device_id=device, device_id_type=MESH,
        )

    def arrived(dst, sem):
        pltpu.make_async_copy(dst, dst, sem).wait()

    plane_peers = [flipped(seq, k) for k in range(1, seq_n)]
    column_peers = [(quarter + j) % groups for j in range(1, groups)]
    partner = {"grp": 1 - grp, "seq": seq, "tp": tp}
    core_mate = flipped(seq, 1)

    barrier = pltpu.get_barrier_semaphore()
    for peer in plane_peers:
        pl.semaphore_signal(barrier, inc=1, device_id=plane(peer), device_id_type=MESH)
    for peer in column_peers:
        pl.semaphore_signal(barrier, inc=1, device_id=column(peer), device_id_type=MESH)
    pl.semaphore_wait(barrier, len(plane_peers) + len(column_peers))

    pending = []

    def go(copy):
        copy.start()
        pending.append(copy)

    mine = lat_all.at[seq, grp]
    go(send(lat.at[0], mine, lat_s.at[0], lat_r.at[grp, seq], partner))
    for k, peer in enumerate(plane_peers):
        go(send(lat.at[0], mine, lat_s.at[k + 1], lat_r.at[grp, seq], plane(peer)))
    lat_all[seq, grp] = lat[0]

    w_aug[0 : 2 * channels, :] = pw[...]
    bias = pb[...]
    b_high, b_middle, b_low = three_parts(bias)
    line = lax.broadcasted_iota(jnp.int32, (16, width), 0)
    extra = jnp.where(line < 6, 1.0, 0.0)
    extra = jnp.where(line == 0, b_high, extra)
    extra = jnp.where(line == 1, b_middle, extra)
    extra = jnp.where(line == 2, b_low, extra)
    w_aug[2 * channels : 2 * channels + 16, :] = extra.astype(BF16)
    rest = w_aug.shape[0] - 2 * channels - 16
    w_aug[2 * channels + 16 :, :] = jnp.zeros((rest, width), BF16)
    w_mean = jnp.sum(pw[...].astype(F32), axis=1, keepdims=True) * (1.0 / width)
    b_mean = jnp.sum(bias, axis=1, keepdims=True) * (1.0 / width)

    other = lat_all.at[seq, 1 - grp]
    arrived(other, lat_r.at[1 - grp, seq])
    for k, peer in enumerate(plane_peers):
        go(send(other, other, lat_f.at[k], lat_r.at[1 - grp, seq], plane(peer)))

    ow_all[seq] = ow[...]
    go(send(ow, ow_all.at[seq], ow_s.at[0], ow_r.at[seq], plane(core_mate)))
    chips = seq_n // 2
    same_core = [flipped(seq, 2 * k) for k in range(1, chips)]
    early = [k for k in range(1, chips) if k & (k - 1) == 0]
    late = [k for k in range(1, chips) if k & (k - 1) != 0]
    for k in early:
        go(send(ow, ow_all.at[seq], ow_s.at[k], ow_r.at[seq], plane(same_core[k - 1])))

    wanted = rows[...]

    def picked(source, total):
        base = lax.broadcasted_iota(jnp.int32, (local, key_n), 0) + source * local
        hot = jnp.where(base == wanted, 1.0, 0.0).astype(BF16)
        block = lat_all[source].reshape(2 * channels, local)
        return total + jnp.dot(block, hot, preferred_element_type=F32)

    x_t = picked(seq, jnp.zeros((2 * channels, key_n), F32))
    for peer in plane_peers:
        arrived(lat_all.at[peer, grp], lat_r.at[grp, peer])
        arrived(lat_all.at[peer, 1 - grp], lat_r.at[1 - grp, peer])
        x_t = picked(peer, x_t)
    mean = jnp.sum(x_t * w_mean, axis=0, keepdims=True) + b_mean
    m_high, m_middle, m_low = three_parts(-mean)
    line = lax.broadcasted_iota(jnp.int32, (x_aug.shape[1] - 2 * channels, key_n), 0)
    extra = jnp.where(line < 3, 1.0, 0.0)
    extra = jnp.where(line == 3, m_high, extra)
    extra = jnp.where(line == 4, m_middle, extra)
    extra = jnp.where(line == 5, m_low, extra)
    x_aug[:, : 2 * channels] = x_t.T.astype(BF16)
    x_aug[:, 2 * channels :] = extra.T.astype(BF16)

    block = centre.shape[0]
    chunk = 1280 if width % 1280 == 0 else width
    mine_ss = ss_all.at[seq]
    key_lines = key_n // 128
    query_lines = query_n // 128
    for b in range(key_n // block):
        has_query = b * block < query_n
        first = 0 if has_query else 1
        x_block = x_aug[b * block : (b + 1) * block, :]

        def embed(c, total):
            at = pl.ds(pl.multiple_of(c * chunk, 128), chunk)
            e = jnp.dot(x_block, w_aug[:, at], preferred_element_type=F32)
            centre[:, at] = e
            sq = e * e
            for i in range(chunk // 128):
                total = total + sq[:, i * 128 : (i + 1) * 128]
            return total

        total = lax.fori_loop(0, width // chunk, embed, jnp.zeros((block, 128), F32))
        spread = jnp.sum(total, axis=1, keepdims=True) * (1.0 / width)
        factor = lax.rsqrt(spread + norm_eps)

        def project(c, total):
            at = pl.ds(pl.multiple_of(c * chunk, 128), chunk)
            normed = centre[:, at] * factor * (1.0 + mod[1:2, at]) + mod[0:1, at]
            weight = jnp.concatenate([wq[i, at, :] for i in range(first, 3)], axis=1)
            return total + jnp.dot(normed.astype(BF16), weight, preferred_element_type=F32)

        raw = lax.fori_loop(
            0, width // chunk, project, jnp.zeros((block, (3 - first) * hd), F32)
        )
        at = slice(b * block, (b + 1) * block)
        if has_query:
            q_raw[at, :] = raw[:, :hd]
        k_raw[at, :] = raw[:, (1 - first) * hd : (2 - first) * hd]
        v_t[:, at] = raw[:, (2 - first) * hd :].T.astype(BF16)

    for i in range(query_lines):
        piece = q_raw[i * 128 : (i + 1) * 128, :]
        mine_ss[i : i + 1, :] = jnp.sum((piece * piece).T, axis=0, keepdims=True)
    for i in range(key_lines):
        piece = k_raw[i * 128 : (i + 1) * 128, :]
        at = query_lines + i
        mine_ss[at : at + 1, :] = jnp.sum((piece * piece).T, axis=0, keepdims=True)
    if ss_all.shape[1] > query_lines + key_lines:
        left = ss_all.shape[1] - query_lines - key_lines
        mine_ss[query_lines + key_lines :, :] = jnp.zeros((left, 128), F32)
    for k, peer in enumerate(plane_peers):
        go(send(mine_ss, mine_ss, ss_s.at[k], ss_r.at[seq], plane(peer)))
    for k in late:
        go(send(ow, ow_all.at[seq], ow_s.at[k], ow_r.at[seq], plane(same_core[k - 1])))
    for peer in plane_peers:
        arrived(ss_all.at[peer], ss_r.at[peer])
    ss_total = ss_all[0]
    for i in range(1, seq_n):
        ss_total = ss_total + ss_all[i]
    inverse = lax.rsqrt(ss_total * (1.0 / (hd * seq_n)) + norm_eps).T
    for i in range(query_lines):
        at = slice(i * 128, (i + 1) * 128)
        piece = q_raw[at, :] * inverse[:, i : i + 1] * gain[0:1, :]
        q_all[quarter, :, at] = piece.T.astype(BF16)
    for j, peer in enumerate(column_peers):
        go(send(q_all.at[quarter], q_all.at[quarter], q_s.at[j], q_r.at[quarter], column(peer)))
    for i in range(key_lines):
        at = slice(i * 128, (i + 1) * 128)
        column_at = query_lines + i
        piece = k_raw[at, :] * inverse[:, column_at : column_at + 1] * gain[1:2, :]
        k_low[at, :] = piece.astype(BF16)

    scale = hd ** (-0.5)

    def attend(index):
        scores = jnp.dot(k_low[...], q_all[index], preferred_element_type=F32) * scale
        top = jnp.max(scores, axis=0, keepdims=True)
        probs = jnp.exp(scores - top)
        total = jnp.sum(probs, axis=0, keepdims=True)
        acc = jnp.dot(v_t[...], probs.astype(BF16), preferred_element_type=F32)
        return top, total, acc

    own = attend(quarter)
    for j, peer in enumerate(column_peers):
        arrived(q_all.at[peer], q_r.at[peer])
        top, total, acc = attend(peer)
        part_acc[j] = acc.astype(BF16)
        go(send(part_acc.at[j], got_acc.at[quarter], acc_s.at[j], acc_r.at[quarter], column(peer)))
        line = lax.broadcasted_iota(jnp.int32, (8, query_n), 0)
        part_stat[j] = jnp.where(line == 0, top, total)
        go(send(part_stat.at[j], got_stat.at[quarter], stat_s.at[j], stat_r.at[quarter], column(peer)))

    def relay(k):
        origin = same_core[k - 1]
        arrived(ow_all.at[origin], ow_r.at[origin])
        go(send(ow_all.at[origin], ow_all.at[origin], ow_l.at[k], ow_r.at[origin], plane(core_mate)))

    for k in early:
        relay(k)

    top, total, acc = own
    for peer in column_peers:
        arrived(got_stat.at[peer], stat_r.at[peer])
        arrived(got_acc.at[peer], acc_r.at[peer])
        peer_top = got_stat[peer, 0:1, :]
        peer_total = got_stat[peer, 1:2, :]
        both = jnp.maximum(top, peer_top)
        mine_factor = jnp.exp(top - both)
        peer_factor = jnp.exp(peer_top - both)
        total = total * mine_factor + peer_total * peer_factor
        acc = acc * mine_factor + got_acc[peer].astype(F32) * peer_factor
        top = both
    attention = (acc / total).T.astype(BF16)
    att_z[pl.ds(quarter * owners, owners)] = attention.reshape(owners, query_n // owners, hd)
    span = att_z.at[pl.ds(quarter * owners, owners)]
    for j, peer in enumerate(column_peers):
        go(send(span, span, az_s.at[j], az_r.at[quarter], column(peer)))

    def give(index):
        for i in range(owners):
            owner = index * owners + i

            @pl.when(owner != seq)
            def _():
                send(
                    att_z.at[owner], att_x.at[seq], ax_s.at[owner], ax_r.at[seq], plane(owner)
                ).start()

            @pl.when(owner == seq)
            def _():
                att_x[seq] = att_z[owner]

    give(quarter)
    for k in late:
        relay(k)
    for peer in column_peers:
        arrived(att_z.at[pl.ds(peer * owners, owners)], az_r.at[peer])
        give(peer)
    arrived(ow_all.at[core_mate], ow_r.at[core_mate])
    for k in range(1, chips):
        origin = flipped(core_mate, 2 * k)
        arrived(ow_all.at[origin], ow_r.at[origin])
    for peer in plane_peers:
        arrived(att_x.at[peer], ax_r.at[peer])
    lhs = jnp.concatenate([att_x[i] for i in range(seq_n)], axis=1)
    step = 256 if cols % 256 == 0 else cols
    for c in range(cols // step):
        at = slice(c * step, (c + 1) * step)
        mixed = jnp.dot(
            lhs, ow_all[:, :, at].reshape(seq_n * hd, step), preferred_element_type=F32
        )
        gate = mod[2:3, pl.ds(pl.multiple_of(quarter * cols + c * step, 128), step)]
        out[:, at] = (mixed * gate).astype(BF16)

    for copy in pending:
        copy.wait_send()
    for owner in range(seq_n):

        @pl.when(owner != seq)
        def _():
            send(
                att_z.at[owner], att_x.at[seq], ax_s.at[owner], ax_r.at[seq], plane(owner)
            ).wait_send()


def per_device(
    latents, patch_weight, patch_bias, modulation, qkv_weight, norm_gain, out_weight,
    token_order, window_start,
):
    seq_n = lax.axis_size("seq")
    tp_n = lax.axis_size("tp")
    groups = lax.axis_size("grp") * tp_n
    quarter = lax.axis_index("grp") * tp_n + lax.axis_index("tp")
    channels, local = latents.shape[1:]
    tokens = local * seq_n
    window = QW_DEV * seq_n
    width = patch_weight.shape[1]
    hd = qkv_weight.shape[2]
    cols = out_weight.shape[1]
    query_n = window // groups
    key_n = tokens // groups
    twice = jnp.concatenate([token_order, token_order])
    ordered = lax.dynamic_slice_in_dim(twice, window_start[0], tokens)
    rest_n = key_n - query_n
    rows = jnp.concatenate(
        [
            lax.dynamic_slice_in_dim(ordered, quarter * query_n, query_n),
            lax.dynamic_slice_in_dim(ordered, window + quarter * rest_n, rest_n),
        ]
    ).reshape(1, key_n)
    depth = 2 * channels + 128
    block = min(256, query_n)
    lines = -(-(key_n // 128 + query_n // 128) // 8) * 8
    dma = pltpu.SemaphoreType.DMA
    vmem = pl.BlockSpec(memory_space=pltpu.VMEM)
    return pl.pallas_call(
        kernel,
        out_shape=jax.ShapeDtypeStruct((QW_DEV, cols), BF16),
        in_specs=[vmem] * 8,
        out_specs=vmem,
        scratch_shapes=[
            pltpu.VMEM((seq_n, 2, channels, local), BF16),
            pltpu.VMEM((key_n, depth), BF16),
            pltpu.VMEM((depth, width), BF16),
            pltpu.VMEM((block, width), F32),
            pltpu.VMEM((query_n, hd), F32),
            pltpu.VMEM((key_n, hd), F32),
            pltpu.VMEM((hd, key_n), BF16),
            pltpu.VMEM((key_n, hd), BF16),
            pltpu.VMEM((seq_n, lines, 128), F32),
            pltpu.VMEM((groups, hd, query_n), BF16),
            pltpu.VMEM((groups - 1, hd, query_n), BF16),
            pltpu.VMEM((groups - 1, 8, query_n), F32),
            pltpu.VMEM((groups, hd, query_n), BF16),
            pltpu.VMEM((groups, 8, query_n), F32),
            pltpu.VMEM((seq_n, QW_DEV, hd), BF16),
            pltpu.VMEM((seq_n, QW_DEV, hd), BF16),
            pltpu.VMEM((seq_n, hd, cols), BF16),
            dma((seq_n,)), dma((seq_n,)), dma((2, seq_n)),
            dma((seq_n,)), dma((seq_n,)), dma((seq_n,)),
            dma((seq_n,)), dma((seq_n,)),
            dma((groups,)), dma((groups,)),
            dma((groups,)), dma((groups,)), dma((groups,)), dma((groups,)),
            dma((groups,)), dma((groups,)),
            dma((seq_n,)), dma((seq_n,)),
        ],
        compiler_params=pltpu.CompilerParams(
            collective_id=0, has_side_effects=True, vmem_limit_bytes=60 * 1024 * 1024
        ),
    )(
        latents,
        patch_weight,
        patch_bias.reshape(1, width),
        modulation,
        jnp.transpose(qkv_weight, (1, 0, 2)),
        norm_gain,
        out_weight,
        rows,
    )


def solution(mesh):
    in_specs = (
        P("grp", None, "seq"),
        P(),
        P(),
        P(),
        P(None, None, "seq"),
        P(None, "seq"),
        P("seq", ("grp", "tp")),
        P(),
        P(),
    )
    out_specs = P("seq", ("grp", "tp"))
    return jax.shard_map(
        per_device, mesh=mesh, in_specs=in_specs, out_specs=out_specs, check_vma=False
    )
```

time: 170 us -> 62.4 us (0.37); the launches traced: 168 us -> 62.1 us
  Pallas kernels: 0 us -> 57.7 us
  blocking collectives: 54.5 us -> 0 us
  waiting for transfers between devices: 50 us -> 0 us
  between operations: 14.3 us -> 0.67 us
  matrix products: 12.7 us -> 0 us
  other arithmetic: 12.6 us -> 0.59 us
  local copies, waits for them, and re-layouts: 15 us -> 3.2 us
  starting transfers between devices: 7.17 us -> 0 us
    pallas_call x0 -> x1, Pallas kernels: none -> 57.7 us  [per_device(): pl.pallas_call(kernel, out_shape=jax.ShapeDtypeStruct((QW_DEV, cols), BF1...]
    all_gather x2 -> x0, waiting for transfers between devices: 43.2 us -> none  [the longest x1 26 us: joined(): everything = jax.tree.map(lambda part: lax.all_gather(part, axis), array)]
    all_gather x4 -> x0, blocking collectives: 43.2 us -> none  [the longest x2 21.4 us: joined(): everything = jax.tree.map(lambda part: lax.all_gather(part, axis), array)]
    dot_general x9 -> x0, matrix products: 12.7 us -> none  [the longest x2 5.05 us: one_block(): return jnp.dot(normed, flat_weight, preferred_element_type=jnp.float32)]
    psum x1 -> x0, blocking collectives: 11.3 us -> none  [per_device(): lax.psum((jnp.sum(query_raw * query_raw, axis=1), jnp.sum(key_raw * key_r...]
    all_to_all x1 -> x0, waiting for transfers between devices: 6.12 us -> none  [per_device(): lax.all_to_all(attention, 'seq', split_axis=0, concat_axis=1, tiled=True)]
    unnamed x27 -> x2, local copies, waits for them, and re-layouts: 7.73 us -> 2.42 us
    all_to_all x1 -> x0, starting transfers between devices: 4.75 us -> none  [per_device(): lax.all_to_all(attention, 'seq', split_axis=0, concat_axis=1, tiled=True)]
  transfers between devices with their start and end apart: 4 -> 0, of which waited for: 3 -> 0; matrix products, arithmetic and copies ran while one was open for 11% -> 0% of each run, Pallas kernels for 0% -> 0%
where the time goes in v1:
time: 62.4 us; the launch traced here: 62.1 us
  Pallas kernels  57.7 us (92%)
  local copies, waits for them, and re-layouts  3.2 us (5%)
  between operations  0.67 us (1%)
    pallas_call x1, Pallas kernels, per_device(): pl.pallas_call(kernel, out_shape=jax.ShapeDtypeStruct((QW_DEV, cols), BF1...  57.7 us
    unnamed x2, local copies, waits for them, and re-layouts  2.42 us

profile of v1, /device:TPU:9, one launch (start us, length us, event | category | flops | bytes accessed | tf_op | source)
XLA Modules:
  0.0 62.1 jit_solution(10962606963906995305)
XLA Ops:
  0.7 0.7 %constant_dynamic-update-slice_fusion.1 = s32[4096]{0:T(1024)S(1)} fusion(s32[2048]{0:T(1024)} %param.16), kind=kLoop, calls=%fused_computation.1 | loop fusion | bytes 16384
  1.4 0.7 %constant_dynamic-update-slice_fusion = s32[4096]{0:T(1024)S(1)} fusion(s32[4096]{0:T(1024)S(1)} %constant_dynamic-update-slice_fusion.1, s32[2048]{0:T(1024)} %param.16), kind=kLoop, calls=%fused_computation | loop fusion | bytes 16384 | tf_op jit(solution)/shard_map/concatenate | solution.py:319
  2.1 0.1 fusion
  2.1 0.6 pad_add_fusion
  2.7 57.7 %shard_map.91 = bf16[128,1280]{1,0:T(8,128)(2,1)} custom-call(bf16[1,64,256]{2,1,0:T(8,128)(2,1)} %lat.1, bf16[128,5120]{1,0:T(8,128)(2,1)} %pw.1, f32[1,5120]{1,0:T(1,128)} %bitcast.8, f32[3,5120]{1,0:T(4,128)} %mod.1, bf16[3,5120,128]{2,1,0:T(8,128)(2,1)} %bitcast.7, f32[2,128]{1,0:T(2,128)} %gain.1, bf16[128,1280]{1,0:T(8,128)(2,1)} %ow.1, s32[1,512]{1,0:T(1,128)} %bitcast.9), custom_call_target="tpu_custom_call" | custom-call | tf_op jit(solution)/shard_map/pallas_call | solution.py:333
  60.4 1.7 %copy.13 = bf16[128,1280]{1,0:T(8,128)(2,1)} copy(bf16[128,1280]{1,0:T(8,128)(2,1)} %shard_map.91) | data formatting | bytes 655360

commit v2 on v1

--- a/solution.py
+++ b/solution.py
@@ -29,10 +29,10 @@
 
 
 def kernel(
-    lat, pw, pb, mod, wq, gain, ow, rows, out,
-    lat_all, x_aug, w_aug, centre, q_raw, k_raw, v_t, k_low,
-    ss_all, q_all, part_acc, part_stat, got_acc, got_stat, att_z, att_x, ow_all,
-    lat_s, lat_f, lat_r, ow_s, ow_l, ow_r, ss_s, ss_r, q_s, q_r,
+    lat, pw, pb, mod, wq_hbm, gain, ow, rows, out,
+    lat_all, x_aug, w_aug, wq, centre, q_raw, k_raw, v_t, k_low,
+    ssq_all, ssk_all, q_all, part_acc, part_stat, got_acc, got_stat, att_z, att_x, ow_all,
+    load, lat_s, lat_f, lat_r, ow_s, ow_l, ow_r, ssq_s, ssq_r, ssk_s, ssk_r, q_s, q_r,
     acc_s, acc_r, stat_s, stat_r, az_s, az_r, ax_s, ax_r,
 ):
     grp, seq, tp = lax.axis_index("grp"), lax.axis_index("seq"), lax.axis_index("tp")
@@ -67,6 +67,13 @@
     partner = {"grp": 1 - grp, "seq": seq, "tp": tp}
     core_mate = flipped(seq, 1)
 
+    pw_load = pltpu.make_async_copy(pw, w_aug.at[pl.ds(0, 2 * channels)], load.at[0])
+    wq_load = pltpu.make_async_copy(wq_hbm, wq, load.at[1])
+    ow_load = pltpu.make_async_copy(ow, ow_all.at[seq], load.at[2])
+    pw_load.start()
+    wq_load.start()
+    ow_load.start()
+
     barrier = pltpu.get_barrier_semaphore()
     for peer in plane_peers:
         pl.semaphore_signal(barrier, inc=1, device_id=plane(peer), device_id_type=MESH)
@@ -86,7 +93,6 @@
         go(send(lat.at[0], mine, lat_s.at[k + 1], lat_r.at[grp, seq], plane(peer)))
     lat_all[seq, grp] = lat[0]
 
-    w_aug[0 : 2 * channels, :] = pw[...]
     bias = pb[...]
     b_high, b_middle, b_low = three_parts(bias)
     line = lax.broadcasted_iota(jnp.int32, (16, width), 0)
@@ -97,7 +103,8 @@
     w_aug[2 * channels : 2 * channels + 16, :] = extra.astype(BF16)
     rest = w_aug.shape[0] - 2 * channels - 16
     w_aug[2 * channels + 16 :, :] = jnp.zeros((rest, width), BF16)
-    w_mean = jnp.sum(pw[...].astype(F32), axis=1, keepdims=True) * (1.0 / width)
+    pw_load.wait()
+    w_mean = jnp.sum(w_aug[0 : 2 * channels, :].astype(F32), axis=1, keepdims=True) * (1.0 / width)
     b_mean = jnp.sum(bias, axis=1, keepdims=True) * (1.0 / width)
 
     other = lat_all.at[seq, 1 - grp]
@@ -105,14 +112,19 @@
     for k, peer in enumerate(plane_peers):
         go(send(other, other, lat_f.at[k], lat_r.at[1 - grp, seq], plane(peer)))
 
-    ow_all[seq] = ow[...]
-    go(send(ow, ow_all.at[seq], ow_s.at[0], ow_r.at[seq], plane(core_mate)))
     chips = seq_n // 2
     same_core = [flipped(seq, 2 * k) for k in range(1, chips)]
     early = [k for k in range(1, chips) if k & (k - 1) == 0]
     late = [k for k in range(1, chips) if k & (k - 1) != 0]
-    for k in early:
-        go(send(ow, ow_all.at[seq], ow_s.at[k], ow_r.at[seq], plane(same_core[k - 1])))
+    half = hd // 2
+
+    def give_weights(ks, h):
+        part = pl.ds(h * half, half)
+        for k in ks:
+            peer = core_mate if k == 0 else same_core[k - 1]
+            go(send(
+                ow.at[part], ow_all.at[seq, part], ow_s.at[h, k], ow_r.at[h, seq], plane(peer)
+            ))
 
     wanted = rows[...]
 
@@ -127,6 +139,7 @@
         arrived(lat_all.at[peer, grp], lat_r.at[grp, peer])
         arrived(lat_all.at[peer, 1 - grp], lat_r.at[1 - grp, peer])
         x_t = picked(peer, x_t)
+    give_weights([0] + early, 0)
     mean = jnp.sum(x_t * w_mean, axis=0, keepdims=True) + b_mean
     m_high, m_middle, m_low = three_parts(-mean)
     line = lax.broadcasted_iota(jnp.int32, (x_aug.shape[1] - 2 * channels, key_n), 0)
@@ -139,9 +152,37 @@
 
     block = centre.shape[0]
     chunk = 1280 if width % 1280 == 0 else width
-    mine_ss = ss_all.at[seq]
     key_lines = key_n // 128
     query_lines = query_n // 128
+
+    def share(raw, lines, everyone, send_sem, recv_sem):
+        for i in range(lines):
+            piece = raw[i * 128 : (i + 1) * 128, :]
+            everyone[seq, i : i + 1, :] = jnp.sum((piece * piece).T, axis=0, keepdims=True)
+        if everyone.shape[1] > lines:
+            everyone[seq, lines:, :] = jnp.zeros((everyone.shape[1] - lines, 128), F32)
+        mine_ss = everyone.at[seq]
+        for k, peer in enumerate(plane_peers):
+            go(send(mine_ss, mine_ss, send_sem.at[k], recv_sem.at[seq], plane(peer)))
+
+    def inverse_of(everyone, recv_sem):
+        for peer in plane_peers:
+            arrived(everyone.at[peer], recv_sem.at[peer])
+        total = everyone[0]
+        for i in range(1, seq_n):
+            total = total + everyone[i]
+        return lax.rsqrt(total * (1.0 / (hd * seq_n)) + norm_eps).T
+
+    def send_queries():
+        inverse = inverse_of(ssq_all, ssq_r)
+        for i in range(query_lines):
+            at = slice(i * 128, (i + 1) * 128)
+            piece = q_raw[at, :] * inverse[:, i : i + 1] * gain[0:1, :]
+            q_all[quarter, :, at] = piece.T.astype(BF16)
+        mine_q = q_all.at[quarter]
+        for j, peer in enumerate(column_peers):
+            go(send(mine_q, mine_q, q_s.at[j], q_r.at[quarter], column(peer)))
+
     for b in range(key_n // block):
         has_query = b * block < query_n
         first = 0 if has_query else 1
@@ -159,6 +200,10 @@
         total = lax.fori_loop(0, width // chunk, embed, jnp.zeros((block, 128), F32))
         spread = jnp.sum(total, axis=1, keepdims=True) * (1.0 / width)
         factor = lax.rsqrt(spread + norm_eps)
+        if b == 0:
+            wq_load.wait()
+        if b * block == query_n:
+            send_queries()
 
         def project(c, total):
             at = pl.ds(pl.multiple_of(c * chunk, 128), chunk)
@@ -175,36 +220,18 @@
         k_raw[at, :] = raw[:, (1 - first) * hd : (2 - first) * hd]
         v_t[:, at] = raw[:, (2 - first) * hd :].T.astype(BF16)
 
-    for i in range(query_lines):
-        piece = q_raw[i * 128 : (i + 1) * 128, :]
-        mine_ss[i : i + 1, :] = jnp.sum((piece * piece).T, axis=0, keepdims=True)
-    for i in range(key_lines):
-        piece = k_raw[i * 128 : (i + 1) * 128, :]
-        at = query_lines + i
-        mine_ss[at : at + 1, :] = jnp.sum((piece * piece).T, axis=0, keepdims=True)
-    if ss_all.shape[1] > query_lines + key_lines:
-        left = ss_all.shape[1] - query_lines - key_lines
-        mine_ss[query_lines + key_lines :, :] = jnp.zeros((left, 128), F32)
-    for k, peer in enumerate(plane_peers):
-        go(send(mine_ss, mine_ss, ss_s.at[k], ss_r.at[seq], plane(peer)))
-    for k in late:
-        go(send(ow, ow_all.at[seq], ow_s.at[k], ow_r.at[seq], plane(same_core[k - 1])))
-    for peer in plane_peers:
-        arrived(ss_all.at[peer], ss_r.at[peer])
-    ss_total = ss_all[0]
-    for i in range(1, seq_n):
-        ss_total = ss_total + ss_all[i]
-    inverse = lax.rsqrt(ss_total * (1.0 / (hd * seq_n)) + norm_eps).T
-    for i in range(query_lines):
-        at = slice(i * 128, (i + 1) * 128)
-        piece = q_raw[at, :] * inverse[:, i : i + 1] * gain[0:1, :]
-        q_all[quarter, :, at] = piece.T.astype(BF16)
-    for j, peer in enumerate(column_peers):
-        go(send(q_all.at[quarter], q_all.at[quarter], q_s.at[j], q_r.at[quarter], column(peer)))
+        if (b + 1) * block == query_n:
+            share(q_raw, query_lines, ssq_all, ssq_s, ssq_r)
+            give_weights([0] + early, 1)
+    if query_n == key_n:
+        send_queries()
+    share(k_raw, key_lines, ssk_all, ssk_s, ssk_r)
+    for h in range(2):
+        give_weights(late, h)
+    inverse = inverse_of(ssk_all, ssk_r)
     for i in range(key_lines):
         at = slice(i * 128, (i + 1) * 128)
-        column_at = query_lines + i
-        piece = k_raw[at, :] * inverse[:, column_at : column_at + 1] * gain[1:2, :]
+        piece = k_raw[at, :] * inverse[:, i : i + 1] * gain[1:2, :]
         k_low[at, :] = piece.astype(BF16)
 
     scale = hd ** (-0.5)
@@ -229,8 +256,10 @@
 
     def relay(k):
         origin = same_core[k - 1]
-        arrived(ow_all.at[origin], ow_r.at[origin])
-        go(send(ow_all.at[origin], ow_all.at[origin], ow_l.at[k], ow_r.at[origin], plane(core_mate)))
+        for h in range(2):
+            part = ow_all.at[origin, pl.ds(h * half, half)]
+            arrived(part, ow_r.at[h, origin])
+            go(send(part, part, ow_l.at[h, k], ow_r.at[h, origin], plane(core_mate)))
 
     for k in early:
         relay(k)
@@ -273,10 +302,11 @@
     for peer in column_peers:
         arrived(att_z.at[pl.ds(peer * owners, owners)], az_r.at[peer])
         give(peer)
-    arrived(ow_all.at[core_mate], ow_r.at[core_mate])
-    for k in range(1, chips):
+    ow_load.wait()
+    for k in range(chips):
         origin = flipped(core_mate, 2 * k)
-        arrived(ow_all.at[origin], ow_r.at[origin])
+        for h in range(2):
+            arrived(ow_all.at[origin, pl.ds(h * half, half)], ow_r.at[h, origin])
     for peer in plane_peers:
         arrived(att_x.at[peer], ax_r.at[peer])
     lhs = jnp.concatenate([att_x[i] for i in range(seq_n)], axis=1)
@@ -316,35 +346,37 @@
     cols = out_weight.shape[1]
     query_n = window // groups
     key_n = tokens // groups
-    twice = jnp.concatenate([token_order, token_order])
-    ordered = lax.dynamic_slice_in_dim(twice, window_start[0], tokens)
     rest_n = key_n - query_n
-    rows = jnp.concatenate(
-        [
-            lax.dynamic_slice_in_dim(ordered, quarter * query_n, query_n),
-            lax.dynamic_slice_in_dim(ordered, window + quarter * rest_n, rest_n),
-        ]
-    ).reshape(1, key_n)
+    start = window_start[0]
+    before = lax.dynamic_slice_in_dim(token_order, quarter * rest_n, rest_n)
+    behind = lax.dynamic_slice_in_dim(token_order, window + quarter * rest_n, rest_n)
+    rest = jnp.where(quarter * rest_n + jnp.arange(rest_n) < start, before, behind)
+    queries = lax.dynamic_slice_in_dim(token_order, start + quarter * query_n, query_n)
+    rows = jnp.concatenate([queries, rest]).reshape(1, key_n)
     depth = 2 * channels + 128
     block = min(256, query_n)
-    lines = -(-(key_n // 128 + query_n // 128) // 8) * 8
+    query_lines = -(-query_n // 1024) * 8
+    key_lines = -(-key_n // 1024) * 8
     dma = pltpu.SemaphoreType.DMA
     vmem = pl.BlockSpec(memory_space=pltpu.VMEM)
+    hbm = pl.BlockSpec(memory_space=pl.ANY)
     return pl.pallas_call(
         kernel,
         out_shape=jax.ShapeDtypeStruct((QW_DEV, cols), BF16),
-        in_specs=[vmem] * 8,
+        in_specs=[vmem, hbm, vmem, vmem, hbm, vmem, hbm, vmem],
         out_specs=vmem,
         scratch_shapes=[
             pltpu.VMEM((seq_n, 2, channels, local), BF16),
             pltpu.VMEM((key_n, depth), BF16),
             pltpu.VMEM((depth, width), BF16),
+            pltpu.VMEM((3, width, hd), BF16),
             pltpu.VMEM((block, width), F32),
             pltpu.VMEM((query_n, hd), F32),
             pltpu.VMEM((key_n, hd), F32),
             pltpu.VMEM((hd, key_n), BF16),
             pltpu.VMEM((key_n, hd), BF16),
-            pltpu.VMEM((seq_n, lines, 128), F32),
+            pltpu.VMEM((seq_n, query_lines, 128), F32),
+            pltpu.VMEM((seq_n, key_lines, 128), F32),
             pltpu.VMEM((groups, hd, query_n), BF16),
             pltpu.VMEM((groups - 1, hd, query_n), BF16),
             pltpu.VMEM((groups - 1, 8, query_n), F32),
@@ -353,9 +385,10 @@
             pltpu.VMEM((seq_n, QW_DEV, hd), BF16),
             pltpu.VMEM((seq_n, QW_DEV, hd), BF16),
             pltpu.VMEM((seq_n, hd, cols), BF16),
+            dma((3,)),
             dma((seq_n,)), dma((seq_n,)), dma((2, seq_n)),
-            dma((seq_n,)), dma((seq_n,)), dma((seq_n,)),
-            dma((seq_n,)), dma((seq_n,)),
+            dma((2, seq_n)), dma((2, seq_n)), dma((2, seq_n)),
+            dma((seq_n,)), dma((seq_n,)), dma((seq_n,)), dma((seq_n,)),
             dma((groups,)), dma((groups,)),
             dma((groups,)), dma((groups,)), dma((groups,)), dma((groups,)),
             dma((groups,)), dma((groups,)),

time: 62.4 us -> 53 us (0.85)
  Pallas kernels: 57.7 us -> 49 us
  local copies, waits for them, and re-layouts: 3.2 us -> 1.72 us
  other arithmetic: 0.59 us -> 1.43 us
    pallas_call x1, Pallas kernels: 57.7 us -> 49 us  [per_device(): pl.pallas_call(kernel, out_shape=jax.ShapeDtypeStruct((QW_DEV, cols), BF1...]
    dynamic_slice x0 -> x1, other arithmetic: none -> 0.85 us  [per_device(): lax.dynamic_slice_in_dim(token_order, start + quarter * query_n, query_n)]
    unnamed x2 -> x1, local copies, waits for them, and re-layouts: 2.42 us -> 1.72 us
    concatenate x1 -> x0, local copies, waits for them, and re-layouts: 0.7 us -> none  [per_device(): twice = jnp.concatenate([token_order, token_order])]
where the time goes in v2:
time: 53 us; the launch traced here: 52.8 us
  Pallas kernels  49 us (92%)
  local copies, waits for them, and re-layouts  1.72 us (3%)
  other arithmetic  1.43 us (3%)
  between operations  0.67 us (1%)
    pallas_call x1, Pallas kernels, per_device(): pl.pallas_call(kernel, out_shape=jax.ShapeDtypeStruct((QW_DEV, cols), BF1...  49 us
    unnamed x1, local copies, waits for them, and re-layouts  1.72 us

profile of v2, /device:TPU:9, one launch (start us, length us, event | category | flops | bytes accessed | tf_op | source)
XLA Modules:
  0.0 52.8 jit_solution(10962097965831323201)
XLA Ops:
  0.7 0.8 %fusion = (s32[256]{0:T(256)S(1)}, s32[256]{0:T(256)S(1)}) fusion(s32[2048]{0:T(1024)} %param.16, s32[]{:T(128)S(6)} %select_n.13, s32[]{:T(128)S(6)} %select_n.15, s32[]{:T(128)S(6)} %select_n.14, s32[]{:T(128)} %bitcast.5, s32[]{:T(128)S(6)} %mul.10), kind=kLoop, calls=%fused_computation.2 | loop fusion | flops 768 | bytes 5140 | tf_op jit(solution)/shard_map/dynamic_slice | solution.py:354
  1.5 0.6 %pad_add_fusion = s32[512]{0:T(512)} fusion(s32[256]{0:T(256)S(1)} %get-tuple-element.6, s32[256]{0:T(256)S(1)} %get-tuple-element.5), kind=kLoop, calls=%fused_computation | loop fusion | flops 512 | bytes 4096 | tf_op jit(solution)/shard_map/concatenate | solution.py:355
  2.1 49.0 %shard_map.91 = bf16[128,1280]{1,0:T(8,128)(2,1)} custom-call(bf16[1,64,256]{2,1,0:T(8,128)(2,1)} %lat.1, bf16[128,5120]{1,0:T(8,128)(2,1)} %pw.1, f32[1,5120]{1,0:T(1,128)} %bitcast.7, f32[3,5120]{1,0:T(4,128)} %mod.1, bf16[3,5120,128]{2,1,0:T(8,128)(2,1)} %bitcast.6, f32[2,128]{1,0:T(2,128)} %gain.1, bf16[128,1280]{1,0:T(8,128)(2,1)} %ow.1, s32[1,512]{1,0:T(1,128)} %bitcast.8), custom_call_target="tpu_custom_call" | custom-call | tf_op jit(solution)/shard_map/pallas_call | solution.py:363
  51.1 1.7 %copy.12 = bf16[128,1280]{1,0:T(8,128)(2,1)} copy(bf16[128,1280]{1,0:T(8,128)(2,1)} %shard_map.91) | data formatting | bytes 655360

commit v3 on v2

--- a/solution.py
+++ b/solution.py
@@ -29,7 +29,7 @@
 
 
 def kernel(
-    lat, pw, pb, mod, wq_hbm, gain, ow, rows, out,
+    lat, pw, pb, mod, wq_hbm, gain, ow, query_rows, rest_rows, out,
     lat_all, x_aug, w_aug, wq, centre, q_raw, k_raw, v_t, k_low,
     ssq_all, ssk_all, q_all, part_acc, part_stat, got_acc, got_stat, att_z, att_x, ow_all,
     load, lat_s, lat_f, lat_r, ow_s, ow_l, ow_r, ssq_s, ssq_r, ssk_s, ssk_r, q_s, q_r,
@@ -126,7 +126,7 @@
                 ow.at[part], ow_all.at[seq, part], ow_s.at[h, k], ow_r.at[h, seq], plane(peer)
             ))
 
-    wanted = rows[...]
+    wanted = jnp.concatenate([query_rows[...], rest_rows[...]], axis=1)
 
     def picked(source, total):
         base = lax.broadcasted_iota(jnp.int32, (local, key_n), 0) + source * local
@@ -352,7 +352,6 @@
     behind = lax.dynamic_slice_in_dim(token_order, window + quarter * rest_n, rest_n)
     rest = jnp.where(quarter * rest_n + jnp.arange(rest_n) < start, before, behind)
     queries = lax.dynamic_slice_in_dim(token_order, start + quarter * query_n, query_n)
-    rows = jnp.concatenate([queries, rest]).reshape(1, key_n)
     depth = 2 * channels + 128
     block = min(256, query_n)
     query_lines = -(-query_n // 1024) * 8
@@ -363,7 +362,7 @@
     return pl.pallas_call(
         kernel,
         out_shape=jax.ShapeDtypeStruct((QW_DEV, cols), BF16),
-        in_specs=[vmem, hbm, vmem, vmem, hbm, vmem, hbm, vmem],
+        in_specs=[vmem, hbm, vmem, vmem, hbm, vmem, hbm, vmem, vmem],
         out_specs=vmem,
         scratch_shapes=[
             pltpu.VMEM((seq_n, 2, channels, local), BF16),
@@ -405,7 +404,8 @@
         jnp.transpose(qkv_weight, (1, 0, 2)),
         norm_gain,
         out_weight,
-        rows,
+        queries.reshape(1, query_n),
+        rest.reshape(1, rest_n),
     )
 
 

time: 53 us -> 53 us (level)
    select_n x0 -> x1, other arithmetic: none -> 1.45 us  [per_device(): jnp.where(quarter * rest_n + jnp.arange(rest_n) < start, before, behind)]
    dynamic_slice x1 -> x0, other arithmetic: 0.85 us -> none  [per_device(): lax.dynamic_slice_in_dim(token_order, start + quarter * query_n, query_n)]
    concatenate x1 -> x0, other arithmetic: 0.59 us -> none  [per_device(): rows = jnp.concatenate([queries, rest]).reshape(1, key_n)]
where the time goes in v3:
time: 53 us; the launch traced here: 52.8 us
  Pallas kernels  49 us (92%)
  local copies, waits for them, and re-layouts  1.72 us (3%)
  other arithmetic  1.45 us (3%)
  between operations  0.67 us (1%)
    pallas_call x1, Pallas kernels, per_device(): pl.pallas_call(kernel, out_shape=jax.ShapeDtypeStruct((QW_DEV, cols), BF1...  49 us
    unnamed x1, local copies, waits for them, and re-layouts  1.72 us
    select_n x1, other arithmetic, per_device(): jnp.where(quarter * rest_n + jnp.arange(rest_n) < start, before, behind)  1.45 us

profile of v3, /device:TPU:9, one launch (start us, length us, event | category | flops | bytes accessed | tf_op | source)
XLA Modules:
  0.0 52.8 jit_solution(16072782521240656111)
XLA Ops:
  0.7 1.4 %compare_select_fusion = (s32[256]{0:T(256)}, s32[256]{0:T(256)}) fusion(s32[2048]{0:T(1024)} %param.16, s32[]{:T(128)S(6)} %select_n.15, s32[]{:T(128)S(6)} %select_n.14, s32[]{:T(128)} %bitcast.6, s32[]{:T(128)S(6)} %mul.10, s32[]{:T(128)S(6)} %select_n.13), kind=kLoop, calls=%fused_computation | loop fusion | flops 768 | bytes 5140 | tf_op jit(solution)/shard_map/jit(_where)/select_n | solution.py:353
  2.1 49.0 %shard_map.91 = bf16[128,1280]{1,0:T(8,128)(2,1)} custom-call(bf16[1,64,256]{2,1,0:T(8,128)(2,1)} %lat.1, bf16[128,5120]{1,0:T(8,128)(2,1)} %pw.1, f32[1,5120]{1,0:T(1,128)} %bitcast.8, f32[3,5120]{1,0:T(4,128)} %mod.1, bf16[3,5120,128]{2,1,0:T(8,128)(2,1)} %bitcast.7, f32[2,128]{1,0:T(2,128)} %gain.1, bf16[128,1280]{1,0:T(8,128)(2,1)} %ow.1, ...), custom_call_target="tpu_custom_call" | custom-call | tf_op jit(solution)/shard_map/pallas_call | solution.py:362
  51.1 1.7 %copy.12 = bf16[128,1280]{1,0:T(8,128)(2,1)} copy(bf16[128,1280]{1,0:T(8,128)(2,1)} %shard_map.91) | data formatting | bytes 655360
